TPU v7x, 32 devices: a whole 2x2x4 slice. The times are simulated.
32 devices in a mesh: dp: 4 (over z), head: 2 (over x), width: 4 (over y, core).
Axes of the slice: x: 2, y: 2, z: 4, core: 2. Of those that a mesh axis runs over, the one named last changes fastest.
Arguments:
- block_in: bfloat16 [4096, 768], P('dp', ('head', 'width')), may hold values from -6 to 6
- segments: int32 [4096], P(('dp', 'head')), may hold values from 0 to 512, as said below
- live_counts: int32 [8], P('dp'), may hold values from 256 to 512, as said below
- norm1_gain: float32 [768], P(('head', 'width')), may hold values from 0.5 to 1.5
- norm1_bias: float32 [768], P(('head', 'width')), may hold values from -3 to 3
- qkv_weight: bfloat16 [768, 3, 768], P('head', None, 'width'), may hold values from -8 to 8
- qv_bias: float32 [2, 768], P(None, 'width'), may hold values from -4 to 4
- out_weight: bfloat16 [768, 768], P('width', 'head'), may hold values from -1 to 1
- out_bias: float32 [768], P(('head', 'width')), may hold values from -4 to 4
- norm2_gain: float32 [768], P(('head', 'width')), may hold values from 0.5 to 1.5
- norm2_bias: float32 [768], P(('head', 'width')), may hold values from -3 to 3
- up_weight: bfloat16 [768, 3072], P('head', 'width'), may hold values from -0.21875 to 0.21875
- up_bias: float32 [3072], P('width'), may hold values from -4 to 4
- down_weight: bfloat16 [3072, 768], P('width', 'head'), may hold values from -0.109375 to 0.109375
- down_bias: float32 [768], P(('head', 'width')), may hold values from -4 to 4
- out_cot: bfloat16 [4096, 768], P('dp', ('head', 'width')), may hold values from -6 to 6
Outputs:
- block_out: bfloat16 [4096, 768], P('dp', ('head', 'width'))
- grad_in: float32 [4096, 768], P('dp', ('head', 'width'))
- grad_norm1_gain: float32 [768], P(('head', 'width'))
- grad_norm1_bias: float32 [768], P(('head', 'width'))
- grad_qkv_weight: float32 [768, 3, 768], P('head', None, 'width')
- grad_qv_bias: float32 [2, 768], P(None, 'width')
- grad_out_weight: float32 [768, 768], P('width', 'head')
- grad_out_bias: float32 [768], P(('head', 'width'))
- grad_norm2_gain: float32 [768], P(('head', 'width'))
- grad_norm2_bias: float32 [768], P(('head', 'width'))
- grad_up_weight: float32 [768, 3072], P('head', 'width')
- grad_up_bias: float32 [3072], P('width')
- grad_down_weight: float32 [3072, 768], P('width', 'head')
- grad_down_bias: float32 [768], P(('head', 'width'))
Inputs may be any that keep to these rules, and one draw needn't show every extreme that they name: `segments`: within a token block the document numbers never fall; live slots come first and carry numbers from 0 up; every slot at or past the block's live count carries 512. `live_counts`: live slots of a token block; some block is full and some holds exactly 256.
All inputs are finite; a program needn't handle non-finite values.
Results may differ from a plain program's by a relative error of at most 0.013.
Values may be sent and summed in bfloat16 or wider, within the bound.
No kernel may reach another device: no remote copies, remote signals or barrier semaphores. Data moves between devices by JAX's collectives and lax.ppermute only.
A program may use at most 64 MiB of HBM per device.

v0:
```python
import jax
import jax.numpy as jnp
from jax import lax
from jax.sharding import PartitionSpec as P

D = 768
HD = 64
norm_eps = 1e-05


def gelu_fn(values):
    return jax.nn.gelu(values, approximate=True)


def moments(first_stat, second_stat):
    return lax.psum((first_stat, second_stat), ("head", "width"))


def widen_rows(narrow_rows):
    return lax.all_gather(narrow_rows, "width", axis=1, tiled=True)


def narrow_sum(partial_rows):
    return lax.psum_scatter(partial_rows, "width", scatter_dimension=1, tiled=True)


def hidden_whole(half_rows):
    return lax.all_gather(half_rows, "head", axis=0, tiled=True)


def norm_forward(rows_f, gain, shift):
    row_sums, row_squares = moments(jnp.sum(rows_f, axis=1), jnp.sum(rows_f * rows_f, axis=1))
    row_mean = row_sums / D
    row_var = row_squares / D - row_mean * row_mean
    inv_std = lax.rsqrt(row_var + norm_eps)[:, None]
    normed = (rows_f - row_mean[:, None]) * inv_std
    return (normed, inv_std, (normed * gain + shift).astype(jnp.bfloat16))


def norm_backward(grad_n, normed, inv_std, gain):
    scaled = grad_n * gain
    first_sum, second_sum = moments(jnp.sum(scaled, axis=1), jnp.sum(scaled * normed, axis=1))
    return inv_std * (scaled - first_sum[:, None] / D - normed * (second_sum[:, None] / D))


def body(
    block_in,
    segments,
    live_counts,
    norm1_gain,
    norm1_bias,
    qkv_weight,
    qv_bias,
    out_weight,
    out_bias,
    norm2_gain,
    norm2_bias,
    up_weight,
    up_bias,
    down_weight,
    down_bias,
    out_cot,
):
    group_rows = block_in.shape[0]
    slot_count = segments.shape[0]
    head_cols = qkv_weight.shape[2]
    local_heads = head_cols // HD
    scale_factor = HD ** (-0.5)
    qkv_flat = qkv_weight.reshape(qkv_weight.shape[0], 3 * head_cols)
    rows_f = block_in.astype(jnp.float32)
    normed1, inv1, n1_b = norm_forward(rows_f, norm1_gain, norm1_bias)
    n1_wide = widen_rows(n1_b)
    picked = n1_wide
    qkv_f = lax.psum_scatter(
        jnp.dot(picked, qkv_flat, preferred_element_type=jnp.float32),
        "head",
        scatter_dimension=0,
        tiled=True,
    )
    qkv_f = qkv_f.reshape(slot_count, 3, head_cols)
    queries = (qkv_f[:, 0] + qv_bias[0]).astype(jnp.bfloat16).reshape(slot_count, local_heads, HD)
    key_rows = qkv_f[:, 1].astype(jnp.bfloat16).reshape(slot_count, local_heads, HD)
    values = (qkv_f[:, 2] + qv_bias[1]).astype(jnp.bfloat16).reshape(slot_count, local_heads, HD)
    slot_pos = jnp.arange(slot_count)
    allowed = (segments[:, None] == segments[None, :]) & (slot_pos[None, :] <= slot_pos[:, None])

    def masked_scores():
        raw = (
            jnp.einsum("qhd,khd->hqk", queries, key_rows, preferred_element_type=jnp.float32)
            * scale_factor
        )
        return jnp.where(allowed[None], raw, -1e30)

    scores = masked_scores()
    peak = jnp.max(scores, axis=-1, keepdims=True)
    log_total = peak + jnp.log(jnp.sum(jnp.exp(scores - peak), axis=-1, keepdims=True))
    probs_b = jnp.exp(scores - log_total).astype(jnp.bfloat16)
    mixed = jnp.einsum("hqk,khd->qhd", probs_b, values, preferred_element_type=jnp.float32).astype(
        jnp.bfloat16
    )
    mixed_flat = mixed.reshape(slot_count, head_cols)
    mixed_all = lax.all_gather(mixed_flat, "head", axis=0, tiled=True)
    resid1 = (
        rows_f
        + narrow_sum(jnp.dot(mixed_all, out_weight, preferred_element_type=jnp.float32))
        + out_bias
    )
    normed2, inv2, n2_b = norm_forward(resid1, norm2_gain, norm2_bias)
    n2_wide = widen_rows(n2_b)
    picked = n2_wide
    pre_act = (
        lax.psum_scatter(
            jnp.dot(picked, up_weight, preferred_element_type=jnp.float32),
            "head",
            scatter_dimension=0,
            tiled=True,
        )
        + up_bias
    )
    hidden = gelu_fn(pre_act).astype(jnp.bfloat16)
    hidden_all = hidden_whole(hidden)
    result = (
        resid1
        + narrow_sum(jnp.dot(hidden_all, down_weight, preferred_element_type=jnp.float32))
        + down_bias
    )
    block_out = result.astype(jnp.bfloat16)
    row_ids = jnp.arange(group_rows)
    owner = row_ids // slot_count
    own_count = jnp.sum(
        jnp.where(
            owner[:, None] == jnp.arange(live_counts.shape[0])[None, :], live_counts[None, :], 0
        ),
        axis=1,
    )
    live = (row_ids % slot_count < own_count)[:, None]
    grad_out = jnp.where(live, out_cot.astype(jnp.float32), 0.0)
    grad_out_wide = widen_rows(grad_out.astype(jnp.bfloat16))
    g_down_w = jnp.einsum(
        "tf,td->fd", hidden_all, grad_out_wide, preferred_element_type=jnp.float32
    )
    g_down_b = jnp.sum(grad_out, axis=0)
    picked = grad_out_wide
    grad_hidden = lax.psum_scatter(
        jnp.einsum("td,fd->tf", picked, down_weight, preferred_element_type=jnp.float32),
        "head",
        scatter_dimension=0,
        tiled=True,
    )
    _, pull_back = jax.vjp(gelu_fn, pre_act)
    grad_pre_b = pull_back(grad_hidden)[0].astype(jnp.bfloat16)
    grad_pre_all = hidden_whole(grad_pre_b)
    g_up_w = jnp.einsum("tc,tf->cf", n2_wide, grad_pre_all, preferred_element_type=jnp.float32)
    g_up_b = jnp.sum(grad_pre_all.astype(jnp.float32), axis=0)
    grad_n2 = narrow_sum(
        jnp.einsum("tf,cf->tc", grad_pre_all, up_weight, preferred_element_type=jnp.float32)
    )
    g_norm2_gain = jnp.sum(grad_n2 * normed2, axis=0)
    g_norm2_bias = jnp.sum(grad_n2, axis=0)
    grad_x1 = grad_out + norm_backward(grad_n2, normed2, inv2, norm2_gain)
    grad_x1_wide = widen_rows(grad_x1.astype(jnp.bfloat16))
    g_out_w = jnp.einsum("tc,td->cd", mixed_all, grad_x1_wide, preferred_element_type=jnp.float32)
    g_out_b = jnp.sum(grad_x1, axis=0)
    picked = grad_x1_wide
    grad_mix = lax.psum_scatter(
        jnp.einsum("td,cd->tc", picked, out_weight, preferred_element_type=jnp.float32),
        "head",
        scatter_dimension=0,
        tiled=True,
    )
    grad_mix = grad_mix.reshape(slot_count, local_heads, HD)
    grad_mix_b = grad_mix.astype(jnp.bfloat16)
    delta = jnp.sum(grad_mix * mixed.astype(jnp.float32), axis=-1).T[:, :, None]
    probs_f = jnp.exp(masked_scores() - log_total)
    probs_again = probs_f.astype(jnp.bfloat16)
    grad_probs = jnp.einsum("qhd,khd->hqk", grad_mix_b, values, preferred_element_type=jnp.float32)
    grad_scores = (probs_f * (grad_probs - delta)).astype(jnp.bfloat16)
    grad_q = (
        jnp.einsum("hqk,khd->qhd", grad_scores, key_rows, preferred_element_type=jnp.float32)
        * scale_factor
    )
    grad_k = (
        jnp.einsum("hqk,qhd->khd", grad_scores, queries, preferred_element_type=jnp.float32)
        * scale_factor
    )
    grad_v = jnp.einsum("hqk,qhd->khd", probs_again, grad_mix_b, preferred_element_type=jnp.float32)
    grad_qkv = (
        jnp.stack([grad_q, grad_k, grad_v], axis=1)
        .reshape(slot_count, 3 * head_cols)
        .astype(jnp.bfloat16)
    )
    grad_qkv_all = lax.all_gather(grad_qkv, "head", axis=0, tiled=True)
    g_qkv_w = jnp.einsum(
        "tc,tf->cf", n1_wide, grad_qkv_all, preferred_element_type=jnp.float32
    ).reshape(qkv_weight.shape)
    column_sums = jnp.sum(grad_qkv_all.astype(jnp.float32), axis=0).reshape(3, head_cols)
    g_qv_b = jnp.stack([column_sums[0], column_sums[2]], axis=0)
    grad_n1 = narrow_sum(
        jnp.einsum("tf,cf->tc", grad_qkv_all, qkv_flat, preferred_element_type=jnp.float32)
    )
    g_norm1_gain = jnp.sum(grad_n1 * normed1, axis=0)
    g_norm1_bias = jnp.sum(grad_n1, axis=0)
    grad_in = grad_x1 + norm_backward(grad_n1, normed1, inv1, norm1_gain)
    summed = lax.psum(
        (
            g_norm1_gain,
            g_norm1_bias,
            g_qkv_w,
            g_qv_b,
            g_out_w,
            g_out_b,
            g_norm2_gain,
            g_norm2_bias,
            g_up_w,
            g_up_b,
            g_down_w,
            g_down_b,
        ),
        "dp",
    )
    return (block_out, grad_in) + tuple(summed)


def solution(mesh):
    return jax.shard_map(
        body,
        mesh=mesh,
        in_specs=(
            P("dp", ("head", "width")),
            P(("dp", "head")),
            P("dp"),
            P(("head", "width")),
            P(("head", "width")),
            P("head", None, "width"),
            P(None, "width"),
            P("width", "head"),
            P(("head", "width")),
            P(("head", "width")),
            P(("head", "width")),
            P("head", "width"),
            P("width"),
            P("width", "head"),
            P(("head", "width")),
            P("dp", ("head", "width")),
        ),
        out_specs=(
            P("dp", ("head", "width")),
            P("dp", ("head", "width")),
            P(("head", "width")),
            P(("head", "width")),
            P("head", None, "width"),
            P(None, "width"),
            P("width", "head"),
            P(("head", "width")),
            P(("head", "width")),
            P(("head", "width")),
            P("head", "width"),
            P("width"),
            P("width", "head"),
            P(("head", "width")),
        ),
        check_vma=False,
    )
```

profile of v0, /device:TPU:0, one launch (start us, length us, event | category | flops | bytes accessed | tf_op | source)
XLA Modules:
  0.0 568.9 jit_solution(2139136913742872445)
XLA Ops:
  8.3 15.4 %all-reduce.3 = (f32[1024]{0:T(1024)S(1)}, f32[1024]{0:T(1024)S(1)}) all-reduce(f32[1024]{0:T(1024)S(1)} %get-tuple-element.25, f32[1024]{0:T(1024)S(1)} %get-tuple-element.24), channel_id=1, replica_groups=mesh['dp'=4,'head'=2,'width'=4] {'head','width'}, use_global_device_ids=true, to_apply=%region_3.0 | all-reduce | flops 2048 | bytes 16384 | tf_op jit(solution)/shard_map/psum | solution.py:16
  24.9 7.2 %all_gather.24 = bf16[1024,384]{0,1:T(8,128)(2,1)S(1)} all-gather(bf16[1024,96]{0,1:T(8,128)(2,1)S(1)} %fusion.21), channel_id=1, replica_groups=mesh['dp'=4,'head'=2,'width'=4] {'width'}, dimensions={1}, use_global_device_ids=true | all-gather | bytes 983040 | tf_op jit(solution)/shard_map/all_gather | solution.py:20
  36.3 34.6 %reduce-scatter.9.cloned.1.call-done = f32[512,576]{0,1:T(8,128)} async-done(((f32[1024,576]{0,1:T(8,128)}), f32[512,576]{0,1:T(8,128)}) %reduce-scatter.9.cloned.1.call-update) | async-done | bytes 1179664 | tf_op jit(solution)/shard_map/reduce_scatter | solution.py:74
  76.7 7.1 %all_gather.25 = bf16[1024,192]{0,1:T(8,128)(2,1)S(1)} all-gather(bf16[512,192]{0,1:T(8,128)(2,1)S(1)} %bitcast.65), channel_id=1, replica_groups=mesh['dp'=4,'head'=2,'width'=4] {'head'}, dimensions={0}, use_global_device_ids=true | all-gather | bytes 589824 | tf_op jit(solution)/shard_map/all_gather | solution.py:102
  85.7 8.6 %all_gather.28 = bf16[1024,384]{0,1:T(8,128)(2,1)S(1)} all-gather(bf16[1024,96]{0,1:T(8,128)(2,1)S(1)} %fusion.30), channel_id=1, replica_groups=mesh['dp'=4,'head'=2,'width'=4] {'width'}, dimensions={1}, use_global_device_ids=true | all-gather | bytes 983040 | tf_op jit(solution)/shard_map/all_gather | solution.py:20
  97.1 16.6 %reduce-scatter.11.cloned.1.call-done = f32[1024,96]{0,1:T(8,128)} async-done(((f32[1024,384]{0,1:T(8,128)}), f32[1024,96]{0,1:T(8,128)}) %reduce-scatter.11.cloned.1.call-update) | async-done | bytes 393232 | tf_op jit(solution)/shard_map/reduce_scatter | solution.py:24
  114.8 13.4 %all-reduce.2 = (f32[1024]{0:T(1024)S(1)}, f32[1024]{0:T(1024)S(1)}) all-reduce(f32[1024]{0:T(1024)S(1)} %get-tuple-element.23, f32[1024]{0:T(1024)S(1)} %get-tuple-element.22), channel_id=1, replica_groups=mesh['dp'=4,'head'=2,'width'=4] {'head','width'}, use_global_device_ids=true, to_apply=%region_11.12 | all-reduce | flops 2048 | bytes 16384 | tf_op jit(solution)/shard_map/psum | solution.py:16
  128.4 7.2 %all_gather.26 = bf16[1024,384]{0,1:T(8,128)(2,1)S(1)} all-gather(bf16[1024,96]{0,1:T(8,128)(2,1)S(1)} %add_convert_fusion.1), channel_id=1, replica_groups=mesh['dp'=4,'head'=2,'width'=4] {'width'}, dimensions={1}, use_global_device_ids=true | all-gather | bytes 983040 | tf_op jit(solution)/shard_map/all_gather | solution.py:20
  139.3 20.2 %reduce-scatter.17.cloned.1.call-done = f32[512,768]{1,0:T(8,128)} async-done(((f32[1024,768]{1,0:T(8,128)}), f32[512,768]{1,0:T(8,128)}) %reduce-scatter.17.cloned.1.call-update) | async-done | bytes 1572880 | tf_op jit(solution)/shard_map/reduce_scatter | solution.py:144
  159.5 45.7 %reduce-scatter.13.cloned.1.call-done = f32[512,768]{1,0:T(8,128)} async-done(((f32[1024,768]{1,0:T(8,128)}), f32[512,768]{1,0:T(8,128)}) %reduce-scatter.13.cloned.1.call-update) | async-done | bytes 1572880 | tf_op jit(solution)/shard_map/reduce_scatter | solution.py:112
  205.1 4.2 fusion.8
  210.0 26.7 %all-gather.6.cloned.1.call-done = bf16[1024,768]{1,0:T(8,128)(2,1)} async-done(((bf16[512,768]{1,0:T(8,128)(2,1)}), bf16[1024,768]{1,0:T(8,128)(2,1)}) %all-gather.6.cloned.1.call-update) | async-done | bytes 1572880 | tf_op jit(solution)/shard_map/all_gather | solution.py:28
  240.1 25.8 %all-gather.4.cloned.1.call-done = bf16[1024,768]{1,0:T(8,128)(2,1)} async-done(((bf16[512,768]{1,0:T(8,128)(2,1)}), bf16[1024,768]{1,0:T(8,128)(2,1)}) %all-gather.4.cloned.1.call-update) | async-done | bytes 1572880 | tf_op jit(solution)/shard_map/all_gather | solution.py:28
  269.6 26.9 %reduce-scatter.19.cloned.1.call-done = f32[1024,96]{0,1:T(8,128)} async-done(((f32[1024,384]{0,1:T(8,128)}), f32[1024,96]{0,1:T(8,128)}) %reduce-scatter.19.cloned.1.call-update) | async-done | bytes 393232 | tf_op jit(solution)/shard_map/reduce_scatter | solution.py:24
  298.3 12.7 %all-reduce.1 = (f32[1024]{0:T(1024)S(1)}, f32[1024]{0:T(1024)S(1)}) all-reduce(f32[1024]{0:T(1024)S(1)} %get-tuple-element.15, f32[1024]{0:T(1024)S(1)} %get-tuple-element.19), channel_id=1, replica_groups=mesh['dp'=4,'head'=2,'width'=4] {'head','width'}, use_global_device_ids=true, to_apply=%region_20.21 | all-reduce | flops 2048 | bytes 16384 | tf_op jit(solution)/shard_map/psum | solution.py:16
  311.0 16.1 %reduce-scatter.15.cloned.1.call-done = f32[1024,96]{0,1:T(8,128)} async-done(((f32[1024,384]{0,1:T(8,128)}), f32[1024,96]{0,1:T(8,128)}) %reduce-scatter.15.cloned.1.call-update) | async-done | bytes 393232 | tf_op jit(solution)/shard_map/reduce_scatter | solution.py:24
  329.8 8.0 %all_gather.30 = bf16[1024,384]{0,1:T(8,128)(2,1)S(1)} all-gather(bf16[1024,96]{0,1:T(8,128)(2,1)S(1)} %convert_element_type.83), channel_id=1, replica_groups=mesh['dp'=4,'head'=2,'width'=4] {'width'}, dimensions={1}, use_global_device_ids=true | all-gather | bytes 983040 | tf_op jit(solution)/shard_map/all_gather | solution.py:20
  339.3 17.9 %reduce-scatter.21.cloned.1.call-done = f32[512,192]{0,1:T(8,128)} async-done(((f32[1024,192]{0,1:T(8,128)}), f32[512,192]{0,1:T(8,128)}) %reduce-scatter.21.cloned.1.call-update) | async-done | bytes 393232 | tf_op jit(solution)/shard_map/reduce_scatter | solution.py:165
  365.2 22.9 %all-gather.8.cloned.1.call-done = bf16[1024,576]{0,1:T(8,128)(2,1)} async-done(((bf16[512,576]{0,1:T(8,128)(2,1)}), bf16[1024,576]{0,1:T(8,128)(2,1)}) %all-gather.8.cloned.1.call-update) | async-done | bytes 1179664 | tf_op jit(solution)/shard_map/all_gather | solution.py:192
  391.5 3.6 fusion.57
  401.9 17.7 %reduce-scatter.23.cloned.1.call-done = f32[1024,96]{0,1:T(8,128)} async-done(((f32[1024,384]{0,1:T(8,128)}), f32[1024,96]{0,1:T(8,128)}) %reduce-scatter.23.cloned.1.call-update) | async-done | bytes 393232 | tf_op jit(solution)/shard_map/reduce_scatter | solution.py:24
  421.0 13.0 %all-reduce.4 = (f32[96]{0:T(128)}, f32[96]{0:T(128)}, f32[2,192]{1,0:T(2,128)}, f32[96]{0:T(128)}, f32[96]{0:T(128)}, /*index=5*/f32[96]{0:T(128)}, f32[768]{0:T(1024)}, f32[96]{0:T(128)}) all-reduce(f32[96]{0:T(128)S(1)} %get-tuple-element.16, f32[96]{0:T(128)S(1)} %get-tuple-element.21, ...), channel_id=1, replica_groups=mesh['dp'=4,'head'=2,'width'=4] {'dp'}, use_global_device_ids=true, to_apply=%region_29.30 | all-reduce | flops 1728 | bytes 13824 | tf_op jit(solution)/shard_map/psum | solution.py:204
  434.0 12.8 %all-reduce = (f32[1024]{0:T(1024)S(1)}, f32[1024]{0:T(1024)S(1)}) all-reduce(f32[1024]{0:T(1024)S(1)} %get-tuple-element.17, f32[1024]{0:T(1024)S(1)} %get-tuple-element.18), channel_id=1, replica_groups=mesh['dp'=4,'head'=2,'width'=4] {'head','width'}, use_global_device_ids=true, to_apply=%region_27.28 | all-reduce | flops 2048 | bytes 16384 | tf_op jit(solution)/shard_map/psum | solution.py:16
  448.7 108.4 %all-reduce.8.cloned.1.call-done = (f32[384,3,192]{0,2,1:T(8,128)}, f32[192,384]{1,0:T(8,128)}, f32[384,768]{1,0:T(8,128)}, f32[768,384]{1,0:T(8,128)}) async-done(((f32[384,3,192]{0,2,1:T(8,128)}, f32[192,384]{1,0:T(8,128)}, f32[384,768]{1,0:T(8,128)}, f32[768,384]{1,0:T(8,128)}), (f32[384,3,192]{0,2,1:T(8,128)}, f32[192,384]{1,0:T(8,128)}, f32[384,768]{1,0:T(8,128)}, ...) | async-done | bytes 3538960 | tf_op jit(solution)/shard_map/psum | solution.py:204
  (173 shorter events, 61.4 us)
Async XLA Ops:
  7.2 129.3 %copy-start = (bf16[384,768]{1,0:T(8,128)(2,1)S(1)}, bf16[384,768]{1,0:T(8,128)(2,1)}, u32[]{:S(2)}) copy-start(bf16[384,768]{1,0:T(8,128)(2,1)} %param.27) | copy-start | bytes 1769476
  7.2 25.8 %copy-start.14 = (bf16[384,3,192]{0,2,1:T(8,128)(2,1)S(1)}, bf16[384,3,192]{0,2,1:T(8,128)(2,1)}, u32[]{:S(2)}) copy-start(bf16[384,3,192]{0,2,1:T(8,128)(2,1)} %param.21) | copy-start | bytes 1327108
  7.2 63.7 %reduce-scatter.9.cloned.1.call-start = ((), (), s32[]{:S(2)}) async-start(), calls=%async_computation.8 | async-start | bytes 3538944 | tf_op jit(solution)/shard_map/reduce_scatter | solution.py:74
  35.2 78.4 %reduce-scatter.11.cloned.1.call-start = ((), (), s32[]{:S(2)}) async-start(), calls=%async_computation.9 | async-start | bytes 1966080 | tf_op jit(solution)/shard_map/reduce_scatter | solution.py:24
  36.0 38.0 %copy-start.26 = (f32[3,64]{1,0:T(4,128)}, f32[3,64]{1,0:T(4,128)S(1)}, u32[]{:S(2)}) copy-start(f32[3,64]{1,0:T(4,128)S(1)} %add.174) | copy-start | bytes 2308
  36.1 38.7 %copy-start.37 = (f32[3,64]{1,0:T(4,128)}, f32[3,64]{1,0:T(4,128)S(1)}, u32[]{:S(2)}) copy-start(f32[3,64]{1,0:T(4,128)S(1)} %add.171) | copy-start | bytes 2308
  36.3 38.5 %copy-start.10 = (pred[512,512]{0,1:T(8,128)(4,1)}, pred[512,512]{0,1:T(8,128)(4,1)S(1)}, u32[]{:S(2)}) copy-start(pred[512,512]{0,1:T(8,128)(4,1)S(1)} %fusion.14) | copy-start | bytes 786436
  85.5 74.0 %reduce-scatter.17.cloned.1.call-start = ((), (), s32[]{:S(2)}) async-start(), calls=%async_computation.13 | async-start | bytes 4718592 | tf_op jit(solution)/shard_map/reduce_scatter | solution.py:144
  97.0 31.2 %copy-start.34 = (f32[96]{0:T(128)S(1)}, f32[96]{0:T(128)}, u32[]{:S(2)}) copy-start(f32[96]{0:T(128)} %param.25) | copy-start | bytes 1156
  97.0 31.2 %copy-start.45 = (f32[96]{0:T(128)S(1)}, f32[96]{0:T(128)}, u32[]{:S(2)}) copy-start(f32[96]{0:T(128)} %param.26) | copy-start | bytes 1156
  97.1 108.1 %reduce-scatter.13.cloned.1.call-start = ((), (), s32[]{:S(2)}) async-start(), calls=%async_computation.10 | async-start | bytes 4718592 | tf_op jit(solution)/shard_map/reduce_scatter | solution.py:112
  139.2 66.0 %copy-start.36 = (f32[768]{0:T(1024)S(1)}, f32[768]{0:T(1024)}, u32[]{:S(2)}) copy-start(f32[768]{0:T(1024)} %param.28) | copy-start | bytes 9220
  139.2 97.5 %all-gather.6.cloned.1.call-start = ((), (), s32[]{:S(2)}) async-start(), calls=%async_computation.14 | async-start | bytes 2359296 | tf_op jit(solution)/shard_map/all_gather | solution.py:28
  209.4 56.5 %all-gather.4.cloned.1.call-start = ((), (), s32[]{:S(2)}) async-start(), calls=%async_computation.11 | async-start | bytes 2359296 | tf_op jit(solution)/shard_map/all_gather | solution.py:28
  209.9 86.5 %reduce-scatter.19.cloned.1.call-start = ((), (), s32[]{:S(2)}) async-start(), calls=%async_computation.15 | async-start | bytes 1966080 | tf_op jit(solution)/shard_map/reduce_scatter | solution.py:24
  240.1 87.0 %reduce-scatter.15.cloned.1.call-start = ((), (), s32[]{:S(2)}) async-start(), calls=%async_computation.12 | async-start | bytes 1966080 | tf_op jit(solution)/shard_map/reduce_scatter | solution.py:24
  269.5 57.6 %copy-start.29 = (pred[1024]{0:T(1024)(128)(4,1)S(1)}, pred[1024]{0:T(1024)(128)(4,1)}, u32[]{:S(2)}) copy-start(pred[1024]{0:T(1024)(128)(4,1)} %copy-done.28) | copy-start | bytes 3076
  269.5 57.6 %copy-start.35 = (f32[96]{0:T(128)S(1)}, f32[96]{0:T(128)}, u32[]{:S(2)}) copy-start(f32[96]{0:T(128)} %param.25) | copy-start | bytes 1156
  269.5 57.6 %copy-start.47 = (f32[96]{0:T(128)S(1)}, f32[96]{0:T(128)}, u32[]{:S(2)}) copy-start(f32[96]{0:T(128)} %param.30) | copy-start | bytes 1156
  269.5 87.7 %reduce-scatter.21.cloned.1.call-start = ((), (), s32[]{:S(2)}) async-start(), calls=%async_computation.16 | async-start | bytes 1179648 | tf_op jit(solution)/shard_map/reduce_scatter | solution.py:165
  339.1 49.0 %all-gather.8.cloned.1.call-start = ((), (), s32[]{:S(2)}) async-start(), calls=%async_computation.17 | async-start | bytes 1769472 | tf_op jit(solution)/shard_map/all_gather | solution.py:192
  365.2 54.5 %reduce-scatter.23.cloned.1.call-start = ((), (), s32[]{:S(2)}) async-start(), calls=%async_computation.18 | async-start | bytes 1966080 | tf_op jit(solution)/shard_map/reduce_scatter | solution.py:24
  391.5 165.6 %all-reduce.8.cloned.1.call-start = ((), (), s32[]{:S(2)}) async-start(), calls=%async_computation.19 | async-start | bytes 7077888 | tf_op jit(solution)/shard_map/psum | solution.py:204
  399.8 21.1 %copy-start.40 = (f32[96]{0:T(128)S(1)}, f32[96]{0:T(128)}, u32[]{:S(2)}) copy-start(f32[96]{0:T(128)} %get-tuple-element.14) | copy-start | bytes 1156
  (36 other events, 237.3 us)
Sparse Core Ops, SparseCore 0:
  35.4 35.5 reduce-scatter.8
  85.6 28.0 reduce-scatter.10
  115.9 43.5 reduce-scatter.16
  161.6 43.5 reduce-scatter.12
  209.5 27.1 all-gather.5
  238.7 27.1 all-gather.3
  268.4 28.0 reduce-scatter.18
  299.0 27.9 reduce-scatter.14
  339.2 18.0 reduce-scatter.20
  365.3 22.7 all-gather.7
  391.6 28.0 reduce-scatter.22
  423.3 133.7 all-reduce.7
where the time goes:
time: 570 us; the launch traced here: 569 us
  waiting for transfers between devices  380 us (67%)
  blocking collectives  106 us (19%)
  matrix products  36.1 us (6%)
  other arithmetic  20.3 us (4%)
  between operations  14.8 us (3%)
  local copies, waits for them, and re-layouts  11.3 us (2%)
    psum x1, waiting for transfers between devices, body(): lax.psum((g_norm1_gain, g_norm1_bias, g_qkv_w, g_qv_b, g_out_w, g_out_b,...  108 us
    reduce_scatter x4, waiting for transfers between devices, narrow_sum(): lax.psum_scatter(partial_rows, 'width', scatter_dimension=1, tiled=True)  77.3 us
    psum x4, blocking collectives, moments(): return lax.psum((first_stat, second_stat), ('head', 'width'))  54.3 us
    all_gather x2, waiting for transfers between devices, hidden_whole(): return lax.all_gather(half_rows, 'head', axis=0, tiled=True)  52.5 us
    reduce_scatter x1, waiting for transfers between devices, body(): lax.psum_scatter(jnp.dot(picked, up_weight, preferred_element_type=jnp.fl...  45.7 us
    reduce_scatter x1, waiting for transfers between devices, body(): lax.psum_scatter(jnp.dot(picked, qkv_flat, preferred_element_type=jnp.flo...  34.6 us
    all_gather x4, blocking collectives, widen_rows(): return lax.all_gather(narrow_rows, 'width', axis=1, tiled=True)  31.1 us
    all_gather x1, waiting for transfers between devices, body(): grad_qkv_all = lax.all_gather(grad_qkv, 'head', axis=0, tiled=True)  22.9 us
  transfers between devices with their start and end apart: 12, of which 12 were waited for; matrix products, arithmetic and copies ran while one was open for 5% of the time, Pallas kernels for 0%

commit v1 on v0

--- a/solution.py
+++ b/solution.py
@@ -8,6 +8,22 @@
 norm_eps = 1e-05
 
 
+def ring_gather(x, axis, dim):
+    ways, here, step = (lax.axis_size(axis), lax.axis_index(axis), x.shape[dim])
+    shape = [n * ways if d == dim else n for d, n in enumerate(x.shape)]
+    full = lax.dynamic_update_slice_in_dim(jnp.zeros(shape, x.dtype), x, here * step, axis=dim)
+    going_up = going_down = x
+    for far in range(1, ways // 2 + 1):
+        going_up = lax.ppermute(going_up, axis, [(d, (d + 1) % ways) for d in range(ways)])
+        full = lax.dynamic_update_slice_in_dim(full, going_up, (here - far) % ways * step, axis=dim)
+        if 2 * far < ways:
+            going_down = lax.ppermute(going_down, axis, [(d, (d - 1) % ways) for d in range(ways)])
+            full = lax.dynamic_update_slice_in_dim(
+                full, going_down, (here + far) % ways * step, axis=dim
+            )
+    return full
+
+
 def gelu_fn(values):
     return jax.nn.gelu(values, approximate=True)
 
@@ -17,7 +33,7 @@
 
 
 def widen_rows(narrow_rows):
-    return lax.all_gather(narrow_rows, "width", axis=1, tiled=True)
+    return ring_gather(narrow_rows, "width", 1)
 
 
 def narrow_sum(partial_rows):

time: 570 us -> 575 us (level)
  blocking collectives: 106 us -> 74.5 us
  waiting for transfers between devices: 380 us -> 410 us
  starting transfers between devices: 0.67 us -> 7.67 us
    ppermute x0 -> x12, waiting for transfers between devices: none -> 37.5 us  [the longest x8 36.8 us: ring_gather(): lax.ppermute(going_up, axis, [(d, (d + 1) % ways) for d in range(ways)])]
    all_gather x4 -> x0, blocking collectives: 31.1 us -> none  [widen_rows(): return lax.all_gather(narrow_rows, 'width', axis=1, tiled=True)]
    ppermute x0 -> x12, starting transfers between devices: none -> 7.17 us  [the longest x4 6.93 us: ring_gather(): lax.ppermute(going_down, axis, [(d, (d - 1) % ways) for d in range(ways)])]
  transfers between devices with their start and end apart: 12 -> 24, of which waited for: 12 -> 21; matrix products, arithmetic and copies ran while one was open for 5% -> 5% of each run, Pallas kernels for 0% -> 0%
where the time goes in v1:
time: 575 us
  waiting for transfers between devices  410 us (71%)
  blocking collectives  74.5 us (13%)
  matrix products  36.1 us (6%)
  other arithmetic  20.4 us (4%)
  between operations  14.9 us (3%)
  local copies, waits for them, and re-layouts  11.4 us (2%)
  starting transfers between devices  7.67 us (1%)
    psum x1, waiting for transfers between devices, body(): lax.psum((g_norm1_gain, g_norm1_bias, g_qkv_w, g_qv_b, g_out_w, g_out_b,...  108 us
    reduce_scatter x4, waiting for transfers between devices, narrow_sum(): lax.psum_scatter(partial_rows, 'width', scatter_dimension=1, tiled=True)  74.5 us
    psum x4, blocking collectives, moments(): return lax.psum((first_stat, second_stat), ('head', 'width'))  54.3 us
    all_gather x2, waiting for transfers between devices, hidden_whole(): return lax.all_gather(half_rows, 'head', axis=0, tiled=True)  52.5 us
    reduce_scatter x1, waiting for transfers between devices, body(): lax.psum_scatter(jnp.dot(picked, up_weight, preferred_element_type=jnp.fl...  45.7 us
    ppermute x8, waiting for transfers between devices, ring_gather(): lax.ppermute(going_up, axis, [(d, (d + 1) % ways) for d in range(ways)])  36.8 us
    reduce_scatter x1, waiting for transfers between devices, body(): lax.psum_scatter(jnp.dot(picked, qkv_flat, preferred_element_type=jnp.flo...  33.3 us
    all_gather x1, waiting for transfers between devices, body(): grad_qkv_all = lax.all_gather(grad_qkv, 'head', axis=0, tiled=True)  22.9 us
  transfers between devices with their start and end apart: 24, of which 21 were waited for; matrix products, arithmetic and copies ran while one was open for 5% of the time, Pallas kernels for 0%

profile of v1, /device:TPU:0, one launch (start us, length us, event | category | flops | bytes accessed | tf_op | source)
XLA Modules:
  0.0 574.7 jit_solution(16809205938326217497)
XLA Ops:
  8.4 15.4 %all-reduce.3 = (f32[1024]{0:T(1024)S(1)}, f32[1024]{0:T(1024)S(1)}) all-reduce(f32[1024]{0:T(1024)S(1)} %get-tuple-element.25, f32[1024]{0:T(1024)S(1)} %get-tuple-element.24), channel_id=1, replica_groups=mesh['dp'=4,'head'=2,'width'=4] {'head','width'}, use_global_device_ids=true, to_apply=%region_3.0 | all-reduce | flops 2048 | bytes 16384 | tf_op jit(solution)/shard_map/psum | solution.py:32
  26.8 4.6 collective-permute-done
  31.4 5.0 collective-permute-done.2
  39.8 33.3 %reduce-scatter.9.cloned.1.call-done = f32[512,576]{0,1:T(8,128)} async-done(((f32[1024,576]{0,1:T(8,128)}), f32[512,576]{0,1:T(8,128)}) %reduce-scatter.9.cloned.1.call-update) | async-done | bytes 1179664 | tf_op jit(solution)/shard_map/reduce_scatter | solution.py:90
  78.9 7.2 %all_gather.12 = bf16[1024,192]{0,1:T(8,128)(2,1)S(1)} all-gather(bf16[512,192]{0,1:T(8,128)(2,1)S(1)} %bitcast.65), channel_id=1, replica_groups=mesh['dp'=4,'head'=2,'width'=4] {'head'}, dimensions={0}, use_global_device_ids=true | all-gather | bytes 589824 | tf_op jit(solution)/shard_map/all_gather | solution.py:118
  94.8 4.4 collective-permute-done.8
  102.0 13.7 %reduce-scatter.11.cloned.1.call-done = f32[1024,96]{0,1:T(8,128)} async-done(((f32[1024,384]{0,1:T(8,128)}), f32[1024,96]{0,1:T(8,128)}) %reduce-scatter.11.cloned.1.call-update) | async-done | bytes 393232 | tf_op jit(solution)/shard_map/reduce_scatter | solution.py:40
  116.9 13.3 %all-reduce.2 = (f32[1024]{0:T(1024)S(1)}, f32[1024]{0:T(1024)S(1)}) all-reduce(f32[1024]{0:T(1024)S(1)} %get-tuple-element.23, f32[1024]{0:T(1024)S(1)} %get-tuple-element.22), channel_id=1, replica_groups=mesh['dp'=4,'head'=2,'width'=4] {'head','width'}, use_global_device_ids=true, to_apply=%region_11.12 | all-reduce | flops 2048 | bytes 16384 | tf_op jit(solution)/shard_map/psum | solution.py:32
  136.7 5.0 collective-permute-done.5
  144.5 17.1 %reduce-scatter.17.cloned.1.call-done = f32[512,768]{1,0:T(8,128)} async-done(((f32[1024,768]{1,0:T(8,128)}), f32[512,768]{1,0:T(8,128)}) %reduce-scatter.17.cloned.1.call-update) | async-done | bytes 1572880 | tf_op jit(solution)/shard_map/reduce_scatter | solution.py:160
  161.6 45.7 %reduce-scatter.13.cloned.1.call-done = f32[512,768]{1,0:T(8,128)} async-done(((f32[1024,768]{1,0:T(8,128)}), f32[512,768]{1,0:T(8,128)}) %reduce-scatter.13.cloned.1.call-update) | async-done | bytes 1572880 | tf_op jit(solution)/shard_map/reduce_scatter | solution.py:128
  212.1 26.7 %all-gather.6.cloned.1.call-done = bf16[1024,768]{1,0:T(8,128)(2,1)} async-done(((bf16[512,768]{1,0:T(8,128)(2,1)}), bf16[1024,768]{1,0:T(8,128)(2,1)}) %all-gather.6.cloned.1.call-update) | async-done | bytes 1572880 | tf_op jit(solution)/shard_map/all_gather | solution.py:44
  242.2 25.8 %all-gather.4.cloned.1.call-done = bf16[1024,768]{1,0:T(8,128)(2,1)} async-done(((bf16[512,768]{1,0:T(8,128)(2,1)}), bf16[1024,768]{1,0:T(8,128)(2,1)}) %all-gather.4.cloned.1.call-update) | async-done | bytes 1572880 | tf_op jit(solution)/shard_map/all_gather | solution.py:44
  271.6 26.9 %reduce-scatter.19.cloned.1.call-done = f32[1024,96]{0,1:T(8,128)} async-done(((f32[1024,384]{0,1:T(8,128)}), f32[1024,96]{0,1:T(8,128)}) %reduce-scatter.19.cloned.1.call-update) | async-done | bytes 393232 | tf_op jit(solution)/shard_map/reduce_scatter | solution.py:40
  300.3 12.7 %all-reduce.1 = (f32[1024]{0:T(1024)S(1)}, f32[1024]{0:T(1024)S(1)}) all-reduce(f32[1024]{0:T(1024)S(1)} %get-tuple-element.15, f32[1024]{0:T(1024)S(1)} %get-tuple-element.19), channel_id=1, replica_groups=mesh['dp'=4,'head'=2,'width'=4] {'head','width'}, use_global_device_ids=true, to_apply=%region_20.21 | all-reduce | flops 2048 | bytes 16384 | tf_op jit(solution)/shard_map/psum | solution.py:32
  313.1 16.1 %reduce-scatter.15.cloned.1.call-done = f32[1024,96]{0,1:T(8,128)} async-done(((f32[1024,384]{0,1:T(8,128)}), f32[1024,96]{0,1:T(8,128)}) %reduce-scatter.15.cloned.1.call-update) | async-done | bytes 393232 | tf_op jit(solution)/shard_map/reduce_scatter | solution.py:40
  333.7 4.8 collective-permute-done.9
  338.6 5.0 collective-permute-done.11
  345.0 17.4 %reduce-scatter.21.cloned.1.call-done = f32[512,192]{0,1:T(8,128)} async-done(((f32[1024,192]{0,1:T(8,128)}), f32[512,192]{0,1:T(8,128)}) %reduce-scatter.21.cloned.1.call-update) | async-done | bytes 393232 | tf_op jit(solution)/shard_map/reduce_scatter | solution.py:181
  371.0 22.9 %all-gather.8.cloned.1.call-done = bf16[1024,576]{0,1:T(8,128)(2,1)} async-done(((bf16[512,576]{0,1:T(8,128)(2,1)}), bf16[1024,576]{0,1:T(8,128)(2,1)}) %all-gather.8.cloned.1.call-update) | async-done | bytes 1179664 | tf_op jit(solution)/shard_map/all_gather | solution.py:208
  407.7 17.7 %reduce-scatter.23.cloned.1.call-done = f32[1024,96]{0,1:T(8,128)} async-done(((f32[1024,384]{0,1:T(8,128)}), f32[1024,96]{0,1:T(8,128)}) %reduce-scatter.23.cloned.1.call-update) | async-done | bytes 393232 | tf_op jit(solution)/shard_map/reduce_scatter | solution.py:40
  426.7 13.0 %all-reduce.4 = (f32[96]{0:T(128)}, f32[96]{0:T(128)}, f32[2,192]{1,0:T(2,128)}, f32[96]{0:T(128)}, f32[96]{0:T(128)}, /*index=5*/f32[96]{0:T(128)}, f32[768]{0:T(1024)}, f32[96]{0:T(128)}) all-reduce(f32[96]{0:T(128)S(1)} %get-tuple-element.16, f32[96]{0:T(128)S(1)} %get-tuple-element.21, ...), channel_id=1, replica_groups=mesh['dp'=4,'head'=2,'width'=4] {'dp'}, use_global_device_ids=true, to_apply=%region_29.30 | all-reduce | flops 1728 | bytes 13824 | tf_op jit(solution)/shard_map/psum | solution.py:220
  439.7 12.8 %all-reduce = (f32[1024]{0:T(1024)S(1)}, f32[1024]{0:T(1024)S(1)}) all-reduce(f32[1024]{0:T(1024)S(1)} %get-tuple-element.17, f32[1024]{0:T(1024)S(1)} %get-tuple-element.18), channel_id=1, replica_groups=mesh['dp'=4,'head'=2,'width'=4] {'head','width'}, use_global_device_ids=true, to_apply=%region_27.28 | all-reduce | flops 2048 | bytes 16384 | tf_op jit(solution)/shard_map/psum | solution.py:32
  454.4 108.4 %all-reduce.8.cloned.1.call-done = (f32[384,3,192]{0,2,1:T(8,128)}, f32[192,384]{1,0:T(8,128)}, f32[384,768]{1,0:T(8,128)}, f32[768,384]{1,0:T(8,128)}) async-done(((f32[384,3,192]{0,2,1:T(8,128)}, f32[192,384]{1,0:T(8,128)}, f32[384,768]{1,0:T(8,128)}, f32[768,384]{1,0:T(8,128)}), (f32[384,3,192]{0,2,1:T(8,128)}, f32[192,384]{1,0:T(8,128)}, f32[384,768]{1,0:T(8,128)}, ...) | async-done | bytes 3538960 | tf_op jit(solution)/shard_map/psum | solution.py:220
  (193 shorter events, 84.9 us)
Async XLA Ops:
  7.2 65.9 %reduce-scatter.9.cloned.1.call-start = ((), (), s32[]{:S(2)}) async-start(), calls=%async_computation.8 | async-start | bytes 3538944 | tf_op jit(solution)/shard_map/reduce_scatter | solution.py:90
  25.0 6.4 %collective-permute-start = (bf16[1024,96]{0,1:T(8,128)(2,1)S(1)}, bf16[1024,96]{0,1:T(8,128)(2,1)S(1)}, u32[]{:S(2)}, u32[]{:S(2)}) collective-permute-start(bf16[1024,96]{0,1:T(8,128)(2,1)S(1)} %get-tuple-element.58), channel_id=1, source_target_pairs={{0,1},{1,2},{2,3},{3,0},{4,5},{5,6},{6,7},{7,4},{8,9},{9,10},{10,1... | collective-permute-start | bytes 589832 | tf_op jit(solution)/shard_map/ppermute | solution.py:17
  25.1 6.3 %collective-permute-start.1 = (bf16[1024,96]{0,1:T(8,128)(2,1)S(1)}, bf16[1024,96]{0,1:T(8,128)(2,1)S(1)}, u32[]{:S(2)}, u32[]{:S(2)}) collective-permute-start(bf16[1024,96]{0,1:T(8,128)(2,1)S(1)} %get-tuple-element.58), channel_id=1, source_target_pairs={{0,3},{1,0},{2,1},{3,2},{4,7},{5,4},{6,5},{7,6},{8,11},{9,8},{10,9... | collective-permute-start | bytes 589832 | tf_op jit(solution)/shard_map/ppermute | solution.py:20
  31.4 5.1 collective-permute-start.2
  38.7 77.0 %reduce-scatter.11.cloned.1.call-start = ((), (), s32[]{:S(2)}) async-start(), calls=%async_computation.9 | async-start | bytes 1966080 | tf_op jit(solution)/shard_map/reduce_scatter | solution.py:40
  87.7 73.9 %reduce-scatter.17.cloned.1.call-start = ((), (), s32[]{:S(2)}) async-start(), calls=%async_computation.13 | async-start | bytes 4718592 | tf_op jit(solution)/shard_map/reduce_scatter | solution.py:160
  88.6 5.5 collective-permute-start.6
  88.7 6.2 %collective-permute-start.7 = (bf16[1024,96]{0,1:T(8,128)(2,1)S(1)}, bf16[1024,96]{0,1:T(8,128)(2,1)S(1)}, u32[]{:S(2)}, u32[]{:S(2)}) collective-permute-start(bf16[1024,96]{0,1:T(8,128)(2,1)S(1)} %get-tuple-element.53), channel_id=1, source_target_pairs={{0,3},{1,0},{2,1},{3,2},{4,7},{5,4},{6,5},{7,6},{8,11},{9,8},{10,9... | collective-permute-start | bytes 589832 | tf_op jit(solution)/shard_map/ppermute | solution.py:20
  94.1 5.1 collective-permute-start.8
  102.0 105.2 %reduce-scatter.13.cloned.1.call-start = ((), (), s32[]{:S(2)}) async-start(), calls=%async_computation.10 | async-start | bytes 4718592 | tf_op jit(solution)/shard_map/reduce_scatter | solution.py:128
  130.6 6.0 %collective-permute-start.3 = (bf16[1024,96]{0,1:T(8,128)(2,1)S(1)}, bf16[1024,96]{0,1:T(8,128)(2,1)S(1)}, u32[]{:S(2)}, u32[]{:S(2)}) collective-permute-start(bf16[1024,96]{0,1:T(8,128)(2,1)S(1)} %get-tuple-element.55), channel_id=1, source_target_pairs={{0,1},{1,2},{2,3},{3,0},{4,5},{5,6},{6,7},{7,4},{8,9},{9,10},{10,1... | collective-permute-start | bytes 589832 | tf_op jit(solution)/shard_map/ppermute | solution.py:17
  130.6 6.0 %collective-permute-start.4 = (bf16[1024,96]{0,1:T(8,128)(2,1)S(1)}, bf16[1024,96]{0,1:T(8,128)(2,1)S(1)}, u32[]{:S(2)}, u32[]{:S(2)}) collective-permute-start(bf16[1024,96]{0,1:T(8,128)(2,1)S(1)} %get-tuple-element.55), channel_id=1, source_target_pairs={{0,3},{1,0},{2,1},{3,2},{4,7},{5,4},{6,5},{7,6},{8,11},{9,8},{10,9... | collective-permute-start | bytes 589832 | tf_op jit(solution)/shard_map/ppermute | solution.py:20
  136.6 5.1 collective-permute-start.5
  144.5 94.3 %all-gather.6.cloned.1.call-start = ((), (), s32[]{:S(2)}) async-start(), calls=%async_computation.14 | async-start | bytes 2359296 | tf_op jit(solution)/shard_map/all_gather | solution.py:44
  211.5 56.5 %all-gather.4.cloned.1.call-start = ((), (), s32[]{:S(2)}) async-start(), calls=%async_computation.11 | async-start | bytes 2359296 | tf_op jit(solution)/shard_map/all_gather | solution.py:44
  212.0 86.5 %reduce-scatter.19.cloned.1.call-start = ((), (), s32[]{:S(2)}) async-start(), calls=%async_computation.15 | async-start | bytes 1966080 | tf_op jit(solution)/shard_map/reduce_scatter | solution.py:40
  242.2 87.0 %reduce-scatter.15.cloned.1.call-start = ((), (), s32[]{:S(2)}) async-start(), calls=%async_computation.12 | async-start | bytes 1966080 | tf_op jit(solution)/shard_map/reduce_scatter | solution.py:40
  271.6 90.8 %reduce-scatter.21.cloned.1.call-start = ((), (), s32[]{:S(2)}) async-start(), calls=%async_computation.16 | async-start | bytes 1179648 | tf_op jit(solution)/shard_map/reduce_scatter | solution.py:181
  331.9 6.6 %collective-permute-start.9 = (bf16[1024,96]{0,1:T(8,128)(2,1)S(1)}, bf16[1024,96]{0,1:T(8,128)(2,1)S(1)}, u32[]{:S(2)}, u32[]{:S(2)}) collective-permute-start(bf16[1024,96]{0,1:T(8,128)(2,1)S(1)} %get-tuple-element.51), channel_id=1, source_target_pairs={{0,1},{1,2},{2,3},{3,0},{4,5},{5,6},{6,7},{7,4},{8,9},{9,10},{10,1... | collective-permute-start | bytes 589832 | tf_op jit(solution)/shard_map/ppermute | solution.py:17
  332.0 6.6 %collective-permute-start.10 = (bf16[1024,96]{0,1:T(8,128)(2,1)S(1)}, bf16[1024,96]{0,1:T(8,128)(2,1)S(1)}, u32[]{:S(2)}, u32[]{:S(2)}) collective-permute-start(bf16[1024,96]{0,1:T(8,128)(2,1)S(1)} %get-tuple-element.51), channel_id=1, source_target_pairs={{0,3},{1,0},{2,1},{3,2},{4,7},{5,4},{6,5},{7,6},{8,11},{9,8},{10,9... | collective-permute-start | bytes 589832 | tf_op jit(solution)/shard_map/ppermute | solution.py:20
  338.5 5.1 collective-permute-start.11
  344.9 48.9 %all-gather.8.cloned.1.call-start = ((), (), s32[]{:S(2)}) async-start(), calls=%async_computation.17 | async-start | bytes 1769472 | tf_op jit(solution)/shard_map/all_gather | solution.py:208
  370.9 54.5 %reduce-scatter.23.cloned.1.call-start = ((), (), s32[]{:S(2)}) async-start(), calls=%async_computation.18 | async-start | bytes 1966080 | tf_op jit(solution)/shard_map/reduce_scatter | solution.py:40
  397.2 165.6 %all-reduce.8.cloned.1.call-start = ((), (), s32[]{:S(2)}) async-start(), calls=%async_computation.19 | async-start | bytes 7077888 | tf_op jit(solution)/shard_map/psum | solution.py:220
  (40 other events, 597.0 us)
Sparse Core Ops, SparseCore 0:
  38.9 34.1 reduce-scatter.8
  87.8 27.9 reduce-scatter.10
  118.0 43.5 reduce-scatter.16
  163.7 43.5 reduce-scatter.12
  211.6 27.1 all-gather.5
  240.8 27.1 all-gather.3
  270.5 28.0 reduce-scatter.18
  301.1 27.9 reduce-scatter.14
  345.0 17.2 reduce-scatter.20
  371.1 22.7 all-gather.7
  397.3 28.0 reduce-scatter.22
  429.1 133.7 all-reduce.7
